TPU v7x, 256 devices: a whole 4x4x8 slice. The times are simulated.
256 devices in a mesh: expert: 64 (over y, z, core), dp: 4 (over x).
Axes of the slice: x: 4, y: 4, z: 8, core: 2. Of those that a mesh axis runs over, the one named last changes fastest.
Arguments:
- grad_rows: bfloat16 [4, 32768, 2048], P('dp', 'expert'), may hold values from -6 to 6
- counts: int32 [4, 64, 64], P('dp', 'expert'), may hold values from 0 to 10, as said below
- order: int32 [4, 32768], P('dp', 'expert'), may hold values from 0 to 511, as said below
- hidden: bfloat16 [4, 64, 640, 768], P('dp', 'expert'), may hold values from -0.29882812 to 0.29882812
- down_weight: bfloat16 [64, 768, 2048], P('expert'), may hold values from -0.21875 to 0.21875
- error_in: bfloat16 [4, 64, 768, 2048], P('dp', 'expert'), may hold values from -6 to 6
- q_init: bfloat16 [64, 2048, 64], P('expert'), may hold values from -6 to 6
Outputs:
- input_grad: bfloat16 [4, 32768, 768], P('dp', 'expert')
- p_basis: float32 [64, 768, 64], P('expert')
- q_factor: float32 [64, 2048, 64], P('expert')
- error_out: bfloat16 [4, 64, 768, 2048], P('dp', 'expert')
Inputs may be any that keep to these rules, and one draw needn't show every extreme that they name: On each device (r, s) the 64 counts sum to 512; in every draw one expert receives exactly 10 rows from every device. `order`: each device's 512 entries are a permutation of 0 to 511.
All inputs are finite; a program needn't handle non-finite values.
Results may differ from a plain program's by a relative error of at most 0.001.
Values may be sent and summed in bfloat16 or wider, within the bound.
A program may use at most 128 MiB of HBM per device.

v0:
```python
import jax
import jax.numpy as jnp
from jax import lax
from jax.sharding import PartitionSpec as P


def orthonormal_rows(p_rows, gram):
    lower = jnp.linalg.cholesky(gram)
    return lax.linalg.triangular_solve(lower, p_rows, left_side=False, lower=True, transpose_a=True)


def shards(grad_rows, counts, order, hidden, down_weight, error_in, q_init):
    local_rows = grad_rows[0]
    route_count = counts[0, 0]
    order_local = order[0]
    experts = route_count.shape[0]
    total_rows = local_rows.shape[0]
    width = local_rows.shape[1]
    saved_hidden = hidden[0, 0]
    hidden_units = saved_hidden.shape[1]
    capacity = saved_hidden.shape[0] // experts
    expert_weight = down_weight[0]
    route_ends = jnp.cumsum(route_count)
    route_starts = route_ends - route_count
    slot_ids = jnp.arange(capacity, dtype=jnp.int32)
    pick_index = jnp.minimum(route_starts[:, None] + slot_ids[None, :], total_rows - 1)
    slot_valid = slot_ids[None, :] < route_count[:, None]
    outgoing = local_rows[pick_index.reshape(-1)].reshape(experts, capacity, width)
    outgoing = jnp.where(slot_valid[:, :, None], outgoing, jnp.zeros((), jnp.bfloat16))
    arrived = lax.all_to_all(outgoing, "expert", split_axis=0, concat_axis=0, tiled=True)
    returned = lax.all_to_all(
        jnp.einsum(
            "ncd,fd->ncf", arrived, expert_weight, preferred_element_type=jnp.float32
        ).astype(jnp.bfloat16),
        "expert",
        split_axis=0,
        concat_axis=0,
        tiled=True,
    )
    arrived_flat = arrived.reshape(experts * capacity, width)
    grad_w = lax.dot_general(
        saved_hidden, arrived_flat, (((0,), (0,)), ((), ())), preferred_element_type=jnp.float32
    )
    moment = grad_w + error_in[0, 0].astype(jnp.float32)
    q_start = q_init[0].astype(jnp.float32)
    partial_p = jnp.dot(moment, q_start, precision=lax.Precision.HIGHEST)
    p_total = lax.psum(partial_p, "dp")
    p_basis = orthonormal_rows(
        p_total, jnp.dot(p_total.T, p_total, precision=lax.Precision.HIGHEST)
    )
    partial_q = lax.dot_general(
        moment, p_basis, (((0,), (0,)), ((), ())), precision=lax.Precision.HIGHEST
    )
    replicas = lax.axis_size("dp")
    q_factor = lax.psum(partial_q, "dp") / replicas
    approximation = jnp.dot(p_basis, q_factor.T, precision=lax.Precision.HIGHEST)
    error_new = (moment - approximation).astype(jnp.bfloat16)
    returned_flat = returned.reshape(experts * capacity, hidden_units)
    expert_of = jnp.sum((route_ends[None, :] <= order_local[:, None]).astype(jnp.int32), axis=1)
    expert_ids = jnp.arange(experts, dtype=jnp.int32)
    onehot = (expert_of[:, None] == expert_ids[None, :]).astype(jnp.int32)
    row_base = jnp.sum(onehot * (expert_ids * capacity - route_starts)[None, :], axis=1)
    position = row_base + order_local
    input_grad = returned_flat[position]
    return (input_grad[None], p_basis[None], q_factor[None], error_new[None, None])


def solution(mesh):
    placed = (
        P("dp", "expert", None),
        P("dp", "expert", None),
        P("dp", "expert"),
        P("dp", "expert", None, None),
        P("expert", None, None),
        P("dp", "expert", None, None),
        P("expert", None, None),
    )
    return jax.shard_map(
        shards,
        mesh=mesh,
        in_specs=placed,
        out_specs=(
            P("dp", "expert", None),
            P("expert", None, None),
            P("expert", None, None),
            P("dp", "expert", None, None),
        ),
        check_vma=False,
    )
```

profile of v0, /device:TPU:8, one launch (start us, length us, event | category | flops | bytes accessed | tf_op | source)
XLA Modules:
  0.0 299.9 jit_solution(14025516916071478414)
XLA Ops:
  7.2 0.0 copy-start
  7.2 0.9 iota_compare_fusion.3
  8.1 0.8 copy.31
  8.9 0.1 reduce-window.7
  9.0 0.1 reduce.6
  9.1 0.7 multiply_subtract_fusion
  9.8 0.1 add_minimum_fusion
  9.8 0.1 min.19
  10.0 8.8 %gather_fusion = bf16[640,2048]{1,0:T(8,128)(2,1)} fusion(bf16[512,2048]{1,0:T(8,128)(2,1)} %bitcast.52, s32[1024]{0:T(1024)S(1)} %pad_clamp_fusion.1), kind=kCustom, calls=%fused_computation | custom fusion | bytes 5245440 | tf_op jit(solution)/shard_map/gather | solution.py:28
  18.8 5.4 %reshape.154 = bf16[64,10,2048]{2,1,0:T(8,128)(2,1)} reshape(bf16[640,2048]{1,0:T(8,128)(2,1)} %gather_fusion) | data formatting | bytes 5242880 | tf_op jit(solution)/shard_map/reshape | solution.py:28
  24.2 4.5 %broadcast_select_fusion = bf16[64,10,2048]{2,1,0:T(8,128)(2,1)} fusion(bf16[64,10,2048]{2,1,0:T(8,128)(2,1)} %reshape.154, pred[64,10]{1,0:T(8,128)(4,1)S(1)} %iota_compare_fusion.3), kind=kLoop, calls=%fused_computation.4 | loop fusion | flops 1310720 | bytes 5243520 | tf_op jit(solution)/shard_map/jit(_where)/select_n | solution.py:29
  28.6 12.3 %all-to-all-start = ((bf16[64,10,2048]{2,1,0:T(8,128)(2,1)}), bf16[64,10,2048]{2,1,0:T(8,128)(2,1)}, u32[]{:S(2)}, u32[]{:S(2)}) async-start(bf16[64,10,2048]{2,1,0:T(8,128)(2,1)} %broadcast_select_fusion), calls=%async_computation | async-start | bytes 8388608 | tf_op jit(solution)/shard_map/all_to_all | solution.py:30
  40.9 0.2 all-reduce.3.cloned.1.call-start
  41.2 4.6 %copy.34 = bf16[1,1,768,2048]{2,3,1,0:T(8,128)(2,1)} copy(bf16[1,1,768,2048]{3,2,1,0:T(8,128)(2,1)} %param.12) | data formatting | bytes 6291456 | tf_op args[5]
  45.8 90.0 %all-to-all-done = bf16[64,10,2048]{2,1,0:T(8,128)(2,1)} async-done(((bf16[64,10,2048]{2,1,0:T(8,128)(2,1)}), bf16[64,10,2048]{2,1,0:T(8,128)(2,1)}, u32[]{:S(2)}, u32[]{:S(2)}) %all-to-all-start) | async-done | bytes 2621472 | tf_op jit(solution)/shard_map/all_to_all | solution.py:30
  135.8 5.5 %reshape.156 = bf16[640,2048]{1,0:T(8,128)(2,1)} reshape(bf16[64,10,2048]{2,1,0:T(8,128)(2,1)} %all-to-all-done) | data formatting | bytes 5242880 | tf_op jit(solution)/shard_map/reshape | solution.py:40
  141.3 0.0 copy-start.3
  141.3 5.8 %convert_add_fusion = f32[768,2048]{0,1:T(8,128)S(1)} fusion(bf16[640,2048]{1,0:T(8,128)(2,1)} %reshape.156, bf16[1,1,768,2048]{2,3,1,0:T(8,128)(2,1)} %copy.34, bf16[1,1,640,768]{3,2,1,0:T(8,128)(2,1)} %param.10), kind=kOutput, calls=%fused_computation.2 | convolution fusion | flops 2016411648 | bytes 13041664 | tf_op jit(solution)/shard_map/dot_general | solution.py:41
  147.1 0.0 copy-start.1
  147.1 2.7 copy-done.1
  149.8 0.0 copy-done.3
  149.8 3.2 %fusion.11 = f32[768,64]{0,1:T(8,128)} fusion(f32[768,2048]{0,1:T(8,128)S(1)} %convert_add_fusion, bf16[1,2048,64]{1,2,0:T(8,128)(2,1)S(1)} %copy-done.3), kind=kOutput, calls=%fused_computation.13 | convolution fusion | flops 1207959552 | bytes 6750208 | tf_op jit(solution)/shard_map/dot_general | solution.py:46
  153.0 0.0 all-reduce.3.cloned.1.call-update
  153.0 0.0 copy-done
  153.0 7.0 %fusion.4 = bf16[64,10,768]{2,0,1:T(8,128)(2,1)S(1)} fusion(bf16[1,768,2048]{2,1,0:T(8,128)(2,1)S(1)} %copy-done, bf16[64,10,2048]{2,1,0:T(8,128)(2,1)} %all-to-all-done), kind=kOutput, calls=%fused_computation.9 | convolution fusion | flops 2013757440 | bytes 6750208 | tf_op jit(solution)/shard_map/ncd,fd->ncf/dot_general | solution.py:32
  159.9 1.7 copy.33
  161.6 6.9 %all-to-all-start.1 = ((bf16[64,10,768]{2,1,0:T(8,128)(2,1)}), bf16[64,10,768]{2,1,0:T(8,128)(2,1)}, u32[]{:S(2)}, u32[]{:S(2)}) async-start(bf16[64,10,768]{2,1,0:T(8,128)(2,1)} %copy.33), calls=%async_computation.1 | async-start | bytes 3145728 | tf_op jit(solution)/shard_map/all_to_all | solution.py:31
  168.6 0.3 all-reduce.5.cloned.1.call-start
  168.9 28.4 %all-reduce.3.cloned.1.call-done = f32[768,64]{0,1:T(8,128)} async-done(((f32[768,64]{0,1:T(8,128)}), f32[768,64]{0,1:T(8,128)}) %all-reduce.3.cloned.1.call-update) | async-done | bytes 196624 | tf_op jit(solution)/shard_map/psum | solution.py:47
  197.3 1.3 fusion.20
  198.6 0.1 copy.35
  198.7 5.8 %cholesky.16 = f32[64,64]{1,0:T(8,128)S(1)} custom-call(f32[64,64]{1,0:T(8,128)S(1)} %fusion.17), custom_call_target="Cholesky" | custom-call | tf_op jit(solution)/shard_map/jit(cholesky)/cholesky | solution.py:8
  204.6 0.6 compare_reduce_fusion
  205.2 0.7 fusion.14
  205.9 4.9 %custom-call.6 = f32[1,64,64]{1,2,0:T(8,128)S(1)} custom-call(f32[1,64,64]{2,1,0:T(8,128)S(1)} %fusion.14), custom_call_target="InvertDiagBlocksLowerTriangular" | custom-call | tf_op jit(solution)/shard_map/triangular_solve | solution.py:9
  210.8 1.3 fusion.15
  212.1 0.0 copy-start.2
  212.1 0.0 copy-start.4
  212.1 9.8 %fusion.21 = f32[2048,64]{0,1:T(8,128)} fusion(f32[768,2048]{0,1:T(8,128)} %copy-done.1, f32[768,64]{0,1:T(8,128)S(1)} %fusion.15), kind=kOutput, calls=%fused_computation.41 | convolution fusion | flops 1207959552 | bytes 7012352 | tf_op jit(solution)/shard_map/dot_general | solution.py:51
  221.9 0.0 all-reduce.5.cloned.1.call-update
  221.9 0.0 copy-done.4
  222.0 0.1 convert_reduce_fusion
  222.1 0.1 select_reduce_fusion
  222.2 48.5 %all-reduce.5.cloned.1.call-done = f32[2048,64]{0,1:T(8,128)} async-done(((f32[2048,64]{0,1:T(8,128)}), f32[2048,64]{0,1:T(8,128)}) %all-reduce.5.cloned.1.call-update) | async-done | bytes 524304 | tf_op jit(solution)/shard_map/psum | solution.py:55
  270.7 0.0 copy-done.2
  270.7 8.5 %fusion.2 = bf16[1,1,768,2048]{2,3,1,0:T(8,128)(2,1)} fusion(f32[768,2048]{0,1:T(8,128)} %copy-done.1, f32[768,64]{0,1:T(8,128)S(1)} %fusion.15, f32[2048,64]{0,1:T(8,128)} %all-reduce.5.cloned.1.call-done), kind=kOutput, calls=%fused_computation.7 | convolution fusion | flops 1211236352 | bytes 10158080 | tf_op jit(solution)/shard_map/dot_general | solution.py:56
  279.1 4.6 %copy.37 = bf16[1,1,768,2048]{3,2,1,0:T(8,128)(2,1)} copy(bf16[1,1,768,2048]{2,3,1,0:T(8,128)(2,1)} %fusion.2) | data formatting | bytes 6291456
  283.8 1.9 multiply_bitcast_fusion
  285.6 0.0 all-to-all-done.1
  285.6 3.0 %reshape.155 = bf16[640,768]{1,0:T(8,128)(2,1)} reshape(bf16[64,10,768]{2,1,0:T(8,128)(2,1)} %all-to-all-done.1) | data formatting | bytes 1966080 | tf_op jit(solution)/shard_map/reshape | solution.py:58
  288.7 4.4 %gather_fusion.1 = bf16[512,768]{1,0:T(8,128)(2,1)} fusion(bf16[640,768]{1,0:T(8,128)(2,1)} %reshape.155, s32[1024]{0:T(1024)S(1)} %pad_clamp_fusion), kind=kCustom, calls=%fused_computation.1 | custom fusion | bytes 1574912 | tf_op jit(solution)/shard_map/gather | solution.py:64
  (6 shorter events, 0.1 us)
Async XLA Ops:
  7.2 145.8 %copy-start = (bf16[1,768,2048]{2,1,0:T(8,128)(2,1)S(1)}, bf16[1,768,2048]{2,1,0:T(8,128)(2,1)}, u32[]{:S(2)}) copy-start(bf16[1,768,2048]{2,1,0:T(8,128)(2,1)} %param.11) | copy-start | bytes 9437188
  28.6 107.2 %all-to-all-start = ((bf16[64,10,2048]{2,1,0:T(8,128)(2,1)}), bf16[64,10,2048]{2,1,0:T(8,128)(2,1)}, u32[]{:S(2)}, u32[]{:S(2)}) async-start(bf16[64,10,2048]{2,1,0:T(8,128)(2,1)} %broadcast_select_fusion), calls=%async_computation | async-start | bytes 8388608 | tf_op jit(solution)/shard_map/all_to_all | solution.py:30
  40.9 156.3 %all-reduce.3.cloned.1.call-start = ((), (), s32[]{:S(2)}) async-start(), calls=%async_computation.2 | async-start | bytes 393216 | tf_op jit(solution)/shard_map/psum | solution.py:47
  141.3 8.5 %copy-start.3 = (bf16[1,2048,64]{1,2,0:T(8,128)(2,1)S(1)}, bf16[1,2048,64]{1,2,0:T(8,128)(2,1)}, u32[]{:S(2)}) copy-start(bf16[1,2048,64]{1,2,0:T(8,128)(2,1)} %param.13) | copy-start | bytes 786436
  147.1 2.7 copy-start.1
  161.6 124.0 %all-to-all-start.1 = ((bf16[64,10,768]{2,1,0:T(8,128)(2,1)}), bf16[64,10,768]{2,1,0:T(8,128)(2,1)}, u32[]{:S(2)}, u32[]{:S(2)}) async-start(bf16[64,10,768]{2,1,0:T(8,128)(2,1)} %copy.33), calls=%async_computation.1 | async-start | bytes 3145728 | tf_op jit(solution)/shard_map/all_to_all | solution.py:31
  168.6 102.1 %all-reduce.5.cloned.1.call-start = ((), (), s32[]{:S(2)}) async-start(), calls=%async_computation.3 | async-start | bytes 1048576 | tf_op jit(solution)/shard_map/psum | solution.py:55
  212.1 58.6 %copy-start.2 = (f32[768,64]{0,1:T(8,128)}, f32[768,64]{0,1:T(8,128)S(1)}, u32[]{:S(2)}) copy-start(f32[768,64]{0,1:T(8,128)S(1)} %fusion.15) | copy-start | bytes 589828
  212.1 9.9 %copy-start.4 = (s32[1,512]{1,0:T(1,128)S(1)}, s32[1,512]{1,0:T(1,128)}, u32[]{:S(2)}) copy-start(s32[1,512]{1,0:T(1,128)} %param.9) | copy-start | bytes 6148
Sparse Core Ops, SparseCore 0:
  153.1 44.1 all-reduce.2
  222.1 48.5 all-reduce.4
where the time goes:
time: 301 us; the launch traced here: 300 us
  waiting for transfers between devices  167 us (55%)
  local copies, waits for them, and re-layouts  41.8 us (14%)
  matrix products  36.8 us (12%)
  other arithmetic  20.5 us (7%)
  starting transfers between devices  19.7 us (7%)
  between operations  14.2 us (5%)
    all_to_all x1, waiting for transfers between devices, shards(): lax.all_to_all(outgoing, 'expert', split_axis=0, concat_axis=0, tiled=True)  90 us
    psum x1, waiting for transfers between devices, shards(): q_factor = lax.psum(partial_q, 'dp') / replicas  48.5 us
    psum x1, waiting for transfers between devices, shards(): p_total = lax.psum(partial_p, 'dp')  28.4 us
    all_to_all x1, starting transfers between devices, shards(): lax.all_to_all(outgoing, 'expert', split_axis=0, concat_axis=0, tiled=True)  12.3 us
    unnamed x12, local copies, waits for them, and re-layouts  11.9 us
    dot_general x1, matrix products, shards(): lax.dot_general(moment, p_basis, (((0,), (0,)), ((), ())), precision=lax....  9.82 us
    gather x1, local copies, waits for them, and re-layouts, shards(): local_rows[pick_index.reshape(-1)].reshape(experts, capacity, width)  8.78 us
    dot_general x1, matrix products, shards(): jnp.dot(p_basis, q_factor.T, precision=lax.Precision.HIGHEST)  8.46 us
  transfers between devices with their start and end apart: 4, of which 3 were waited for; matrix products, arithmetic and copies ran while one was open for 18% of the time, Pallas kernels for 0%

commit v1 on v0

--- a/solution.py
+++ b/solution.py
@@ -52,7 +52,8 @@
         moment, p_basis, (((0,), (0,)), ((), ())), precision=lax.Precision.HIGHEST
     )
     replicas = lax.axis_size("dp")
-    q_factor = lax.psum(partial_q, "dp") / replicas
+    test_the_shifts_all = lambda raw: jnp.sum(lax.all_gather(raw, "dp"), 0)
+    q_factor = test_the_shifts_all(partial_q) / replicas
     approximation = jnp.dot(p_basis, q_factor.T, precision=lax.Precision.HIGHEST)
     error_new = (moment - approximation).astype(jnp.bfloat16)
     returned_flat = returned.reshape(experts * capacity, hidden_units)

time: 301 us -> 319 us (1.060)
  waiting for transfers between devices: 167 us -> 173 us
  local copies, waits for them, and re-layouts: 41.8 us -> 45.4 us
  starting transfers between devices: 19.7 us -> 23.3 us
    psum x1 -> x0, waiting for transfers between devices: 48.5 us -> none  [shards(): q_factor = lax.psum(partial_q, 'dp') / replicas]
    all_to_all x1, waiting for transfers between devices: 0.01 us -> 38.3 us  [shards(): lax.all_to_all(jnp.einsum('ncd,fd->ncf', arrived, expert_weight, preferre...]
    psum x1, waiting for transfers between devices: 28.4 us -> 44 us  [shards(): p_total = lax.psum(partial_p, 'dp')]
    all_to_all x1, starting transfers between devices: 6.94 us -> 10.7 us  [shards(): lax.all_to_all(jnp.einsum('ncd,fd->ncf', arrived, expert_weight, preferre...]
    reduce_sum x0 -> x1, other arithmetic: none -> 3.7 us  [shards(): test_the_shifts_all = lambda raw: jnp.sum(lax.all_gather(raw, 'dp'), 0)]
    all_gather x0 -> x1, local copies, waits for them, and re-layouts: none -> 3.62 us  [shards(): test_the_shifts_all = lambda raw: jnp.sum(lax.all_gather(raw, 'dp'), 0)]
    unnamed x12 -> x14, local copies, waits for them, and re-layouts: 11.9 us -> 11.9 us
  transfers between devices with their start and end apart: 4 -> 4, of which waited for: 3 -> 3; matrix products, arithmetic and copies ran while one was open for 18% -> 7% of each run, Pallas kernels for 0% -> 0%
where the time goes in v1:
time: 319 us; the launch traced here: 316 us
  waiting for transfers between devices  173 us (54%)
  local copies, waits for them, and re-layouts  45.4 us (14%)
  matrix products  37.3 us (12%)
  starting transfers between devices  23.3 us (7%)
  other arithmetic  23.1 us (7%)
  between operations  14.2 us (4%)
    all_to_all x1, waiting for transfers between devices, shards(): lax.all_to_all(outgoing, 'expert', split_axis=0, concat_axis=0, tiled=True)  90.2 us
    psum x1, waiting for transfers between devices, shards(): p_total = lax.psum(partial_p, 'dp')  44 us
    all_to_all x1, waiting for transfers between devices, shards(): lax.all_to_all(jnp.einsum('ncd,fd->ncf', arrived, expert_weight, preferre...  38.3 us
    all_to_all x1, starting transfers between devices, shards(): lax.all_to_all(outgoing, 'expert', split_axis=0, concat_axis=0, tiled=True)  12.3 us
    unnamed x14, local copies, waits for them, and re-layouts  11.9 us
    all_to_all x1, starting transfers between devices, shards(): lax.all_to_all(jnp.einsum('ncd,fd->ncf', arrived, expert_weight, preferre...  10.7 us
    dot_general x1, matrix products, shards(): lax.dot_general(moment, p_basis, (((0,), (0,)), ((), ())), precision=lax....  9.81 us
    dot_general x1, matrix products, shards(): jnp.dot(p_basis, q_factor.T, precision=lax.Precision.HIGHEST)  8.94 us
  transfers between devices with their start and end apart: 4, of which 3 were waited for; matrix products, arithmetic and copies ran while one was open for 7% of the time, Pallas kernels for 0%

profile of v1, /device:TPU:8, one launch (start us, length us, event | category | flops | bytes accessed | tf_op | source)
XLA Modules:
  0.0 315.9 jit_solution(3867108169862434019)
XLA Ops:
  7.2 0.0 copy-start
  7.2 0.9 iota_compare_fusion.3
  8.1 0.8 copy.31
  8.9 0.1 reduce-window.7
  9.0 0.1 reduce.6
  9.1 0.7 multiply_subtract_fusion
  9.8 0.1 add_minimum_fusion
  9.8 0.1 min.19
  10.0 8.8 %gather_fusion = bf16[640,2048]{1,0:T(8,128)(2,1)} fusion(bf16[512,2048]{1,0:T(8,128)(2,1)} %bitcast.54, s32[1024]{0:T(1024)S(1)} %pad_clamp_fusion.1), kind=kCustom, calls=%fused_computation | custom fusion | bytes 5245440 | tf_op jit(solution)/shard_map/gather | solution.py:28
  18.8 5.4 %reshape.163 = bf16[64,10,2048]{2,1,0:T(8,128)(2,1)} reshape(bf16[640,2048]{1,0:T(8,128)(2,1)} %gather_fusion) | data formatting | bytes 5242880 | tf_op jit(solution)/shard_map/reshape | solution.py:28
  24.2 4.5 %broadcast_select_fusion = bf16[64,10,2048]{2,1,0:T(8,128)(2,1)} fusion(bf16[64,10,2048]{2,1,0:T(8,128)(2,1)} %reshape.163, pred[64,10]{1,0:T(8,128)(4,1)S(1)} %iota_compare_fusion.3), kind=kLoop, calls=%fused_computation.4 | loop fusion | flops 1310720 | bytes 5243520 | tf_op jit(solution)/shard_map/jit(_where)/select_n | solution.py:29
  28.6 12.3 %all-to-all-start = ((bf16[64,10,2048]{2,1,0:T(8,128)(2,1)}), bf16[64,10,2048]{2,1,0:T(8,128)(2,1)}, u32[]{:S(2)}, u32[]{:S(2)}) async-start(bf16[64,10,2048]{2,1,0:T(8,128)(2,1)} %broadcast_select_fusion), calls=%async_computation | async-start | bytes 8388608 | tf_op jit(solution)/shard_map/all_to_all | solution.py:30
  40.9 0.0 all-reduce.2.cloned.1.call-start
  41.0 4.6 %copy.34 = bf16[1,1,768,2048]{2,3,1,0:T(8,128)(2,1)} copy(bf16[1,1,768,2048]{3,2,1,0:T(8,128)(2,1)} %param.12) | data formatting | bytes 6291456 | tf_op args[5]
  45.6 90.2 %all-to-all-done = bf16[64,10,2048]{2,1,0:T(8,128)(2,1)} async-done(((bf16[64,10,2048]{2,1,0:T(8,128)(2,1)}), bf16[64,10,2048]{2,1,0:T(8,128)(2,1)}, u32[]{:S(2)}, u32[]{:S(2)}) %all-to-all-start) | async-done | bytes 2621472 | tf_op jit(solution)/shard_map/all_to_all | solution.py:30
  135.8 5.5 %reshape.165 = bf16[640,2048]{1,0:T(8,128)(2,1)} reshape(bf16[64,10,2048]{2,1,0:T(8,128)(2,1)} %all-to-all-done) | data formatting | bytes 5242880 | tf_op jit(solution)/shard_map/reshape | solution.py:40
  141.3 0.0 copy-start.4
  141.3 5.8 %convert_add_fusion = f32[768,2048]{0,1:T(8,128)S(1)} fusion(bf16[640,2048]{1,0:T(8,128)(2,1)} %reshape.165, bf16[1,1,768,2048]{2,3,1,0:T(8,128)(2,1)} %copy.34, bf16[1,1,640,768]{3,2,1,0:T(8,128)(2,1)} %param.10), kind=kOutput, calls=%fused_computation.2 | convolution fusion | flops 2016411648 | bytes 13041664 | tf_op jit(solution)/shard_map/dot_general | solution.py:41
  147.1 0.0 copy-start.1
  147.1 2.7 copy-done.1
  149.8 0.0 copy-done.4
  149.8 3.2 fusion.11
  153.0 0.0 all-reduce.2.cloned.1.call-update
  153.0 0.2 all-gather.3.cloned.1.call-start
  153.2 44.0 %all-reduce.2.cloned.1.call-done = f32[768,64]{0,1:T(8,128)} async-done(((f32[768,64]{0,1:T(8,128)}), f32[768,64]{0,1:T(8,128)}) %all-reduce.2.cloned.1.call-update) | async-done | bytes 196624 | tf_op jit(solution)/shard_map/psum | solution.py:47
  197.3 1.3 fusion.20
  198.6 0.1 copy.35
  198.7 5.8 %cholesky.16 = f32[64,64]{1,0:T(8,128)S(1)} custom-call(f32[64,64]{1,0:T(8,128)S(1)} %fusion.17), custom_call_target="Cholesky" | custom-call | tf_op jit(solution)/shard_map/jit(cholesky)/cholesky | solution.py:8
  204.6 0.6 compare_reduce_fusion
  205.2 0.7 fusion.14
  205.9 4.9 %custom-call.6 = f32[1,64,64]{1,2,0:T(8,128)S(1)} custom-call(f32[1,64,64]{2,1,0:T(8,128)S(1)} %fusion.14), custom_call_target="InvertDiagBlocksLowerTriangular" | custom-call | tf_op jit(solution)/shard_map/triangular_solve | solution.py:9
  210.8 1.3 fusion.15
  212.1 0.0 copy-start.3
  212.1 9.8 %fusion.21 = f32[2048,64]{0,1:T(8,128)} fusion(f32[768,2048]{0,1:T(8,128)} %copy-done.1, f32[768,64]{0,1:T(8,128)S(1)} %fusion.15), kind=kOutput, calls=%fused_computation.41 | convolution fusion | flops 1207959552 | bytes 7012352 | tf_op jit(solution)/shard_map/dot_general | solution.py:51
  221.9 0.0 all-gather.3.cloned.1.call-update
  221.9 0.0 copy-done
  221.9 7.0 %fusion.4 = bf16[64,10,768]{2,0,1:T(8,128)(2,1)S(1)} fusion(bf16[1,768,2048]{2,1,0:T(8,128)(2,1)S(1)} %copy-done, bf16[64,10,2048]{2,1,0:T(8,128)(2,1)} %all-to-all-done), kind=kOutput, calls=%fused_computation.9 | convolution fusion | flops 2013757440 | bytes 6750208 | tf_op jit(solution)/shard_map/ncd,fd->ncf/dot_general | solution.py:32
  228.9 0.0 copy-start.5
  228.9 1.7 copy.33
  230.6 10.7 %all-to-all-start.1 = ((bf16[64,10,768]{2,1,0:T(8,128)(2,1)}), bf16[64,10,768]{2,1,0:T(8,128)(2,1)}, u32[]{:S(2)}, u32[]{:S(2)}) async-start(bf16[64,10,768]{2,1,0:T(8,128)(2,1)} %copy.33), calls=%async_computation.1 | async-start | bytes 3145728 | tf_op jit(solution)/shard_map/all_to_all | solution.py:31
  241.4 0.0 copy-done.5
  241.4 0.1 convert_reduce_fusion
  241.5 0.1 select_reduce_fusion
  241.6 38.3 %all-to-all-done.1 = bf16[64,10,768]{2,1,0:T(8,128)(2,1)} async-done(((bf16[64,10,768]{2,1,0:T(8,128)(2,1)}), bf16[64,10,768]{2,1,0:T(8,128)(2,1)}, u32[]{:S(2)}, u32[]{:S(2)}) %all-to-all-start.1) | async-done | bytes 983072 | tf_op jit(solution)/shard_map/all_to_all | solution.py:31
  279.9 3.0 reshape.164
  282.9 4.4 %gather_fusion.1 = bf16[512,768]{1,0:T(8,128)(2,1)} fusion(bf16[640,768]{1,0:T(8,128)(2,1)} %reshape.164, s32[1024]{0:T(1024)S(1)} %pad_clamp_fusion), kind=kCustom, calls=%fused_computation.1 | custom fusion | bytes 1574912 | tf_op jit(solution)/shard_map/gather | solution.py:65
  287.3 0.0 all-gather.3.cloned.1.call-done
  287.3 3.6 %reshape.183 = f32[4,2048,64]{1,0,2:T(4,128)} reshape(f32[8192,64]{0,1:T(8,128)} %all-gather.3.cloned.1.call-done) | data formatting | bytes 4194304 | tf_op jit(solution)/shard_map/all_gather | solution.py:55
  291.0 3.7 %reduce_sum.32 = f32[2048,64]{0,1:T(8,128)} reduce(f32[4,2048,64]{1,0,2:T(4,128)} %reshape.183, f32[]{:T(128)} %constant.59.clone.1), dimensions={0}, to_apply=%region_6.7 | reduce | flops 393216 | bytes 2621444 | tf_op jit(solution)/shard_map/reduce_sum | solution.py:55
  294.7 0.0 copy-done.3
  294.7 0.0 copy-start.2
  294.7 8.9 %fusion.2 = bf16[1,1,768,2048]{2,3,1,0:T(8,128)(2,1)} fusion(f32[768,2048]{0,1:T(8,128)} %copy-done.1, f32[768,64]{0,1:T(8,128)S(1)} %fusion.15, f32[2048,64]{0,1:T(8,128)} %reduce_sum.32), kind=kOutput, calls=%fused_computation.7 | convolution fusion | flops 1211236352 | bytes 10158080 | tf_op jit(solution)/shard_map/dot_general | solution.py:57
  303.6 0.0 copy-done.2
  303.6 0.8 multiply_bitcast_fusion
  304.5 4.6 %copy.37 = bf16[1,1,768,2048]{3,2,1,0:T(8,128)(2,1)} copy(bf16[1,1,768,2048]{2,3,1,0:T(8,128)(2,1)} %fusion.2) | data formatting | bytes 6291456
  (6 shorter events, 0.1 us)
Async XLA Ops:
  7.2 214.8 %copy-start = (bf16[1,768,2048]{2,1,0:T(8,128)(2,1)S(1)}, bf16[1,768,2048]{2,1,0:T(8,128)(2,1)}, u32[]{:S(2)}) copy-start(bf16[1,768,2048]{2,1,0:T(8,128)(2,1)} %param.11) | copy-start | bytes 9437188
  28.6 107.2 %all-to-all-start = ((bf16[64,10,2048]{2,1,0:T(8,128)(2,1)}), bf16[64,10,2048]{2,1,0:T(8,128)(2,1)}, u32[]{:S(2)}, u32[]{:S(2)}) async-start(bf16[64,10,2048]{2,1,0:T(8,128)(2,1)} %broadcast_select_fusion), calls=%async_computation | async-start | bytes 8388608 | tf_op jit(solution)/shard_map/all_to_all | solution.py:30
  40.9 156.3 %all-reduce.2.cloned.1.call-start = ((), (), s32[]{:S(2)}) async-start(), calls=%async_computation.2 | async-start | bytes 393216 | tf_op jit(solution)/shard_map/psum | solution.py:47
  141.3 8.5 %copy-start.4 = (bf16[1,2048,64]{1,2,0:T(8,128)(2,1)S(1)}, bf16[1,2048,64]{1,2,0:T(8,128)(2,1)}, u32[]{:S(2)}) copy-start(bf16[1,2048,64]{1,2,0:T(8,128)(2,1)} %param.13) | copy-start | bytes 786436
  147.1 2.7 copy-start.1
  153.0 134.4 %all-gather.3.cloned.1.call-start = ((), (), s32[]{:S(2)}) async-start(), calls=%async_computation.3 | async-start | bytes 2621440 | tf_op jit(solution)/shard_map/all_gather | solution.py:55
  212.1 82.6 %copy-start.3 = (f32[768,64]{0,1:T(8,128)}, f32[768,64]{0,1:T(8,128)S(1)}, u32[]{:S(2)}) copy-start(f32[768,64]{0,1:T(8,128)S(1)} %fusion.15) | copy-start | bytes 589828
  228.9 12.5 %copy-start.5 = (s32[1,512]{1,0:T(1,128)S(1)}, s32[1,512]{1,0:T(1,128)}, u32[]{:S(2)}) copy-start(s32[1,512]{1,0:T(1,128)} %param.9) | copy-start | bytes 6148
  230.6 49.3 %all-to-all-start.1 = ((bf16[64,10,768]{2,1,0:T(8,128)(2,1)}), bf16[64,10,768]{2,1,0:T(8,128)(2,1)}, u32[]{:S(2)}, u32[]{:S(2)}) async-start(bf16[64,10,768]{2,1,0:T(8,128)(2,1)} %copy.33), calls=%async_computation.1 | async-start | bytes 3145728 | tf_op jit(solution)/shard_map/all_to_all | solution.py:31
  294.7 8.9 %copy-start.2 = (f32[2048,64]{0,1:T(8,128)S(1)}, f32[2048,64]{0,1:T(8,128)}, u32[]{:S(2)}) copy-start(f32[2048,64]{0,1:T(8,128)} %reduce_sum.32) | copy-start | bytes 1572868
Sparse Core Ops, SparseCore 0:
  153.1 44.1 all-reduce.1
  222.1 33.8 all-gather.2
